TPU v7x, 32 devices: a whole 2x2x4 slice. The times are simulated.
32 devices in a mesh: coord: 8 (over z, y), cohort: 4 (over x, core).
Axes of the slice: x: 2, y: 2, z: 4, core: 2. Of those that a mesh axis runs over, the one named last changes fastest.
Arguments:
- shapes: bfloat16 [4, 1024, 32768], P('cohort', None, 'coord'), may hold values from -6 to 6
- sketch_signs: int32 [4, 1024, 128], P('cohort'), may hold values from -1 to 1
- merge_sketch: float32 [2, 2, 128, 128], replicated, may hold values from -1.5 to 1.5
Outputs:
- basis: float32 [4, 32768, 128], P('cohort', 'coord')
- scores: float32 [4, 1024, 128], P('cohort', 'coord')
All inputs are finite; a program needn't handle non-finite values.
Results may differ from a plain program's by a relative error of at most 0.0086.
Values sent between devices are 32-bit elements; how exact they have to be, the bound alone decides.
A program may use at most 64 MiB of HBM per device.

v0:
```python
import functools
import math

import jax
import jax.numpy as jnp
from jax import lax
from jax.experimental import pallas as pl
from jax.experimental.pallas import tpu as pltpu
from jax.sharding import PartitionSpec as P

LEVELS = 2
HIGHEST = lax.Precision.HIGHEST
MESH = pl.DeviceIdType.MESH
VMEM = pl.BlockSpec(memory_space=pltpu.VMEM)


def peers_of(n, pair):
    coord = lax.axis_index("coord")
    if not pair:
        return coord, n, lambda rank: {"coord": rank}
    cohort = lax.axis_index("cohort")
    side = lax.rem(cohort, 2)
    base = cohort - side
    rank = coord * 2 + side
    return rank, 2 * n, lambda r: {"coord": r // 2, "cohort": base + lax.rem(r, 2)}


def enter(me, size, ident):
    barrier = pltpu.get_barrier_semaphore()
    for d in range(1, size):
        pl.semaphore_signal(
            barrier, inc=1, device_id=ident(lax.rem(me + d, size)), device_id_type=MESH
        )
    pl.semaphore_wait(barrier, size - 1)


def scatter_sum(part_ref, recv, me, size, ident, send, got):
    copies = []
    for d in range(1, size):
        peer = lax.rem(me + d, size)
        copies.append(
            pltpu.make_async_remote_copy(
                src_ref=part_ref.at[peer],
                dst_ref=recv.at[d],
                send_sem=send.at[d],
                recv_sem=got.at[d],
                device_id=ident(peer),
                device_id_type=MESH,
            )
        )
    for copy in copies:
        copy.start()
    total = part_ref[me]
    for d in range(1, size):
        copies[d - 1].wait_recv()
        total = total + recv[d]
    return total, copies


def all_sum_kernel(n, pair, part_ref, out_ref, recv, send, got, send2, got2):
    me, size, ident = peers_of(n, pair)
    enter(me, size, ident)
    total, copies = scatter_sum(part_ref, recv, me, size, ident, send, got)
    out_ref[me] = total
    spread = []
    for d in range(1, size):
        spread.append(
            pltpu.make_async_remote_copy(
                src_ref=out_ref.at[me],
                dst_ref=out_ref.at[me],
                send_sem=send2.at[d],
                recv_sem=got2.at[d],
                device_id=ident(lax.rem(me + d, size)),
                device_id_type=MESH,
            )
        )
    for copy in spread:
        copy.start()
    for copy in spread:
        copy.wait_recv()
    for copy in copies + spread:
        copy.wait_send()


def all_sum(part, n, pair, ident):
    size = 2 * n if pair else n
    rows, cols = part.shape
    shape = (size, rows // size, cols)
    out = pl.pallas_call(
        functools.partial(all_sum_kernel, n, pair),
        out_shape=jax.ShapeDtypeStruct(shape, part.dtype),
        in_specs=[VMEM],
        out_specs=VMEM,
        scratch_shapes=[pltpu.VMEM(shape, part.dtype)] + [pltpu.SemaphoreType.DMA((size,))] * 4,
        compiler_params=pltpu.CompilerParams(collective_id=ident, has_side_effects=True),
        name=f"all_sum_{ident}",
    )(part.reshape(shape))
    return out.reshape(rows, cols)


def score_kernel(n, scale, part_ref, out_ref, recv, send, got):
    me, size, ident = peers_of(n, False)
    enter(me, size, ident)
    total, copies = scatter_sum(part_ref, recv, me, size, ident, send, got)
    out_ref[...] = total * scale
    for copy in copies:
        copy.wait_send()


def score_sum(part, n, scale, ident):
    rows, cols = part.shape
    shape = (n, rows // n, cols)
    return pl.pallas_call(
        functools.partial(score_kernel, n, scale),
        out_shape=jax.ShapeDtypeStruct(shape[1:], part.dtype),
        in_specs=[VMEM],
        out_specs=VMEM,
        scratch_shapes=[pltpu.VMEM(shape, part.dtype)] + [pltpu.SemaphoreType.DMA((n,))] * 2,
        compiler_params=pltpu.CompilerParams(collective_id=ident, has_side_effects=True),
        name="score_sum",
    )(part.reshape(shape))


def inverse_of(g_ref, x_ref):
    size = g_ref.shape[0]
    step = 8
    tiles = size // step
    lane = lax.broadcasted_iota(jnp.int32, (step, size), 1)
    sub = lax.broadcasted_iota(jnp.int32, (step, size), 0)

    def full(x):
        return jnp.broadcast_to(x, (step, size))

    def total(terms):
        while len(terms) > 1:
            terms = [terms[i] + terms[i + 1] for i in range(0, len(terms), 2)]
        return terms[0]

    left = [g_ref[t * step : (t + 1) * step, :] for t in range(tiles)]
    right = [(lane == sub + t * step).astype(jnp.float32) for t in range(tiles)]
    for t in range(tiles):
        at = t * step
        cols = [full(left[t][:, at + k : at + k + 1]) for k in range(step)]
        e = [[full(cols[k][i : i + 1, :]) for k in range(i + 1)] for i in range(step)]
        rows = [full(left[t][i : i + 1, :]) for i in range(step)]
        rows_x = [full(right[t][i : i + 1, :]) for i in range(step)]
        f = {}
        inv = []
        for s in range(step):
            inv.append(1.0 / e[s][s])
            for i in range(s + 1, step):
                f[i, s] = e[i][s] * inv[s]
                for k in range(s + 1, i + 1):
                    e[i][k] = e[i][k] - f[i, s] * e[k][s]
            for i in range(s + 1, step):
                rows[i] = rows[i] - f[i, s] * rows[s]
                rows_x[i] = rows_x[i] - f[i, s] * rows_x[s]
        out = rows_x[0] * lax.rsqrt(e[0][0])
        for s in range(1, step):
            out = jnp.where(sub == s, rows_x[s] * lax.rsqrt(e[s][s]), out)
        x_ref[at : at + step, :] = out
        rows = [rows[s] * inv[s] for s in range(step)]
        rows_x = [rows_x[s] * inv[s] for s in range(step)]
        for u in range(t + 1, tiles):
            c = [full(left[u][:, at + s : at + s + 1]) for s in range(step)]
            for s in range(step):
                for r in range(s):
                    c[s] = c[s] - f[s, r] * c[r]
            left[u] = left[u] - total([c[s] * rows[s] for s in range(step)])
            right[u] = right[u] - total([c[s] * rows_x[s] for s in range(step)])


def map_kernel(g_ref, mix_ref, out_ref, x_ref):
    inverse_of(g_ref, x_ref)
    out_ref[...] = lax.dot_general(
        x_ref[...],
        mix_ref[...],
        (((0,), (0,)), ((), ())),
        precision=HIGHEST,
        preferred_element_type=jnp.float32,
    )


def lower_inverse(gram):
    return pl.pallas_call(
        inverse_of,
        out_shape=jax.ShapeDtypeStruct(gram.shape, gram.dtype),
        in_specs=[VMEM],
        out_specs=VMEM,
        name="lower_inverse",
    )(gram)


def mixing_map(gram, mix):
    return pl.pallas_call(
        map_kernel,
        out_shape=jax.ShapeDtypeStruct(gram.shape, gram.dtype),
        in_specs=[VMEM, VMEM],
        out_specs=VMEM,
        scratch_shapes=[pltpu.VMEM(gram.shape, gram.dtype)],
        name="mixing_map",
    )(gram, mix)


def sketch_kernel(shapes_ref, signs_ref, centered_ref, sketch_ref, turned):
    @pl.when(pl.program_id(0) == 0)
    def _():
        turned[...] = signs_ref[...].astype(jnp.float32).T.astype(jnp.bfloat16)

    data = shapes_ref[...].astype(jnp.float32)
    mean = jnp.sum(data, axis=0, keepdims=True) * (1.0 / data.shape[0])
    centered = (data - mean).astype(jnp.bfloat16)
    centered_ref[...] = centered
    sketch_ref[...] = jnp.dot(turned[...], centered, preferred_element_type=jnp.float32).T


def center_and_sketch(shapes, signs):
    subjects, coords = shapes.shape
    width = signs.shape[1]
    tile = math.gcd(coords, 512)
    return pl.pallas_call(
        sketch_kernel,
        grid=(coords // tile,),
        out_shape=(
            jax.ShapeDtypeStruct((subjects, coords), jnp.bfloat16),
            jax.ShapeDtypeStruct((coords, width), jnp.float32),
        ),
        in_specs=[
            pl.BlockSpec((subjects, tile), lambda i: (0, i)),
            pl.BlockSpec((subjects, width), lambda i: (0, 0)),
        ],
        out_specs=(
            pl.BlockSpec((subjects, tile), lambda i: (0, i)),
            pl.BlockSpec((tile, width), lambda i: (i, 0)),
        ),
        scratch_shapes=[pltpu.VMEM((width, subjects), jnp.bfloat16)],
        name="center_and_sketch",
    )(shapes, signs)


def project_kernel(side_ref, centered_ref, basis_ref, *rest):
    out_ref = rest[-1]

    @pl.when(pl.program_id(0) == 0)
    def _():
        out_ref[...] = rest[0][...] if len(rest) > 1 else jnp.zeros_like(out_ref)

    out_ref[...] += jnp.dot(
        centered_ref[...], basis_ref[...].astype(jnp.bfloat16), preferred_element_type=jnp.float32
    )


def project(side, centered, basis, start=None):
    subjects = centered.shape[0]
    half, width = basis.shape
    tile = math.gcd(half, 1024)
    steps = half // tile
    extra = [] if start is None else [start]
    whole = pl.BlockSpec((subjects, width), lambda i, side: (0, 0))
    return pl.pallas_call(
        project_kernel,
        grid_spec=pltpu.PrefetchScalarGridSpec(
            num_scalar_prefetch=1,
            grid=(steps,),
            in_specs=[
                pl.BlockSpec((subjects, tile), lambda i, side: (0, side[0] * steps + i)),
                pl.BlockSpec((tile, width), lambda i, side: (i, 0)),
            ]
            + [whole] * len(extra),
            out_specs=whole,
        ),
        out_shape=jax.ShapeDtypeStruct((subjects, width), jnp.float32),
        cost_estimate=pl.CostEstimate(
            flops=2 * subjects * half * width, bytes_accessed=2 * subjects * half, transcendentals=0
        ),
        name="project",
    )(side.reshape(1), centered, basis, *extra)


def gram_of(rows):
    return lax.dot_general(rows, rows, (((0,), (0,)), ((), ())), precision=HIGHEST)


def times_t(a, b):
    return lax.dot_general(a, b, (((1,), (1,)), ((), ())), precision=HIGHEST)


def mix(own, own_map, other, other_map):
    return jnp.matmul(own, own_map, precision=HIGHEST) + jnp.matmul(
        other, other_map, precision=HIGHEST
    )


def swap(value, distance):
    size = lax.axis_size("cohort")
    return lax.ppermute(value, "cohort", [(i, i ^ distance) for i in range(size)])


def on_device(shapes, sketch_signs, merge_sketch):
    n = lax.axis_size("coord")
    position = lax.axis_index("cohort")
    side = position % 2
    upper = position // 2 % 2
    centered, sketch = center_and_sketch(shapes[0], sketch_signs[0])

    half = sketch.shape[0] // 2
    mine = lax.dynamic_slice_in_dim(sketch, side * half, half, 0)
    theirs = swap(lax.dynamic_slice_in_dim(sketch, (1 - side) * half, half, 0), 1)
    own_map = mixing_map(all_sum(gram_of(sketch), n, False, 0), merge_sketch[0][side])
    mine = mix(mine, own_map, theirs, swap(own_map, 1))

    theirs = swap(mine, 2)
    own_map = mixing_map(all_sum(gram_of(mine), n, True, 1), merge_sketch[1][upper])
    mine = mix(mine, own_map, theirs, swap(own_map, 2))

    own_half = times_t(mine, lower_inverse(all_sum(gram_of(mine), n, True, 2)))
    other_half = swap(own_half, 1)
    partial = project(side, centered, own_half)
    partial = project(1 - side, centered, other_half, partial)
    first = jnp.where(side == 1, other_half, own_half)
    second = jnp.where(side == 1, own_half, other_half)
    current = jnp.concatenate([first, second], axis=0)

    width = current.shape[1]
    total_coords = current.shape[0] * n
    scores = score_sum(partial, n, 4.0 * math.sqrt(width / total_coords), 3)
    basis_out = current * math.sqrt(total_coords)
    return (basis_out[None], scores[None])


def solution(mesh):
    placed = (P("cohort", None, "coord"), P("cohort", None, None), P())
    return jax.shard_map(
        on_device,
        mesh=mesh,
        in_specs=placed,
        out_specs=(P("cohort", "coord", None), P("cohort", "coord", None)),
        check_vma=False,
    )
```

profile of v0, /device:TPU:12, one launch (start us, length us, event | category | flops | bytes accessed | tf_op | source)
XLA Modules:
  0.0 123.8 jit_solution(5541717340802426805)
XLA Ops:
  0.6 10.6 %center_and_sketch.1 = (bf16[1024,4096]{1,0:T(8,128)(2,1)}, f32[4096,128]{1,0:T(8,128)}) custom-call(bf16[1024,4096]{1,0:T(8,128)(2,1)} %bitcast.37, s32[1024,128]{1,0:T(8,128)} %bitcast.39), custom_call_target="tpu_custom_call" | custom-call | tf_op jit(solution)/shard_map/center_and_sketch/pallas_call | solution.py:221
  11.3 0.0 copy-start
  11.3 2.5 %constant_dynamic-slice_fusion = f32[2048,128]{1,0:T(8,128)} fusion(f32[4096,128]{1,0:T(8,128)} %get-tuple-element.4, s32[]{:T(128)S(6)} %select_n.43), kind=kLoop, calls=%fused_computation.11 | loop fusion | bytes 2097156 | tf_op jit(solution)/shard_map/dynamic_slice | solution.py:308
  13.8 0.0 collective-permute-start
  13.8 0.0 copy-done
  13.8 0.0 copy-start.5
  13.8 4.1 %fusion.4 = f32[128,128]{1,0:T(8,128)} fusion(f32[4096,128]{1,0:T(8,128)S(1)} %copy-done), kind=kOutput, calls=%fused_computation.14 | convolution fusion | flops 805306368 | bytes 2162688 | tf_op jit(solution)/shard_map/dot_general | solution.py:281
  17.9 13.1 %all_sum_0.1 = f32[8,16,128]{2,1,0:T(8,128)} custom-call(f32[8,16,128]{2,1,0:T(8,128)} %bitcast.40), custom_call_target="tpu_custom_call" | custom-call | tf_op jit(solution)/shard_map/all_sum_0/pallas_call | solution.py:89
  31.0 0.0 copy-done.5
  31.1 0.6 dynamic-slice_bitcast_fusion.1.mix_ref
  31.7 6.1 %mixing_map.2 = f32[128,128]{1,0:T(8,128)} custom-call(f32[128,128]{1,0:T(8,128)} %bitcast.42, f32[128,128]{1,0:T(8,128)} %dynamic-slice_bitcast_fusion.1.mix_ref), custom_call_target="tpu_custom_call" | custom-call | tf_op jit(solution)/shard_map/mixing_map/pallas_call | solution.py:195
  37.8 0.0 collective-permute-start.1
  37.8 1.8 %fusion = f32[2048,128]{1,0:T(8,128)S(1)} fusion(f32[128,128]{1,0:T(8,128)} %mixing_map.2, f32[4096,128]{1,0:T(8,128)S(1)} %copy-done, s32[]{:T(128)S(6)} %select_n.41), kind=kOutput, calls=%fused_computation.7 | convolution fusion | flops 402653184 | bytes 2162692 | tf_op jit(solution)/shard_map/dot_general | solution.py:289
  39.6 0.0 collective-permute-done.1
  39.6 0.0 collective-permute-done
  39.6 1.0 convolution_add_fusion.1
  40.6 1.6 %collective-permute-start.2 = (f32[2048,128]{1,0:T(8,128)S(1)}, f32[2048,128]{1,0:T(8,128)S(1)}, u32[]{:S(2)}, u32[]{:S(2)}) collective-permute-start(f32[2048,128]{1,0:T(8,128)S(1)} %convolution_add_fusion.1), channel_id=1, source_target_pairs={{0,2},{1,3},{2,0},{3,1},{4,6},{5,7},{6,4},{7,5},{8,10},{9,11},{10,... | collective-permute-start | bytes 3145736 | tf_op jit(solution)/shard_map/ppermute | solution.py:296
  42.2 0.6 dynamic-slice_bitcast_fusion.mix_ref
  42.8 2.5 %convolution_bitcast_fusion.1.part_ref = f32[16,8,128]{2,1,0:T(8,128)} fusion(f32[2048,128]{1,0:T(8,128)S(1)} %convolution_add_fusion.1), kind=kOutput, calls=%fused_computation.4 | convolution fusion | flops 402653184 | bytes 1114112 | tf_op jit(solution)/shard_map/dot_general | solution.py:281
  45.2 12.4 %all_sum_1.1 = f32[16,8,128]{2,1,0:T(8,128)} custom-call(f32[16,8,128]{2,1,0:T(8,128)} %convolution_bitcast_fusion.1.part_ref), custom_call_target="tpu_custom_call" | custom-call | tf_op jit(solution)/shard_map/all_sum_1/pallas_call | solution.py:89
  57.6 6.1 %mixing_map.3 = f32[128,128]{1,0:T(8,128)} custom-call(f32[128,128]{1,0:T(8,128)} %bitcast.43, f32[128,128]{1,0:T(8,128)} %dynamic-slice_bitcast_fusion.mix_ref), custom_call_target="tpu_custom_call" | custom-call | tf_op jit(solution)/shard_map/mixing_map/pallas_call | solution.py:195
  63.7 0.5 collective-permute-start.3
  64.3 1.8 %fusion.5 = f32[2048,128]{1,0:T(8,128)S(1)} fusion(f32[2048,128]{1,0:T(8,128)S(1)} %convolution_add_fusion.1, f32[128,128]{1,0:T(8,128)} %mixing_map.3), kind=kOutput, calls=%fused_computation.15 | convolution fusion | flops 402653184 | bytes 2162688 | tf_op jit(solution)/shard_map/dot_general | solution.py:289
  66.1 2.1 %collective-permute-done.3 = f32[128,128]{1,0:T(8,128)S(1)} collective-permute-done((f32[128,128]{1,0:T(8,128)}, f32[128,128]{1,0:T(8,128)S(1)}, u32[]{:S(2)}, u32[]{:S(2)}) %collective-permute-start.3) | collective-permute-done | bytes 65568 | tf_op jit(solution)/shard_map/ppermute | solution.py:296
  68.2 0.0 collective-permute-done.2
  68.2 1.0 convolution_add_fusion
  69.2 2.5 %convolution_bitcast_fusion.part_ref = f32[16,8,128]{2,1,0:T(8,128)} fusion(f32[2048,128]{1,0:T(8,128)S(1)} %convolution_add_fusion), kind=kOutput, calls=%fused_computation.3 | convolution fusion | flops 402653184 | bytes 1114112 | tf_op jit(solution)/shard_map/dot_general | solution.py:281
  71.6 13.2 %all_sum_2.1 = f32[16,8,128]{2,1,0:T(8,128)} custom-call(f32[16,8,128]{2,1,0:T(8,128)} %convolution_bitcast_fusion.part_ref), custom_call_target="tpu_custom_call" | custom-call | tf_op jit(solution)/shard_map/all_sum_2/pallas_call | solution.py:89
  84.9 5.9 %lower_inverse.1 = f32[128,128]{1,0:T(8,128)} custom-call(f32[128,128]{1,0:T(8,128)} %bitcast.44), custom_call_target="tpu_custom_call" | custom-call | tf_op jit(solution)/shard_map/lower_inverse/pallas_call | solution.py:185
  90.7 1.8 %fusion.6.basis_ref = f32[2048,128]{1,0:T(8,128)S(1)} fusion(f32[2048,128]{1,0:T(8,128)S(1)} %convolution_add_fusion, f32[128,128]{1,0:T(8,128)} %lower_inverse.1), kind=kOutput, calls=%fused_computation.16 | convolution fusion | flops 402653184 | bytes 2162688 | tf_op jit(solution)/shard_map/dot_general | solution.py:285
  92.6 0.0 copy-start.1
  92.6 0.2 collective-permute-start.4
  92.8 0.9 copy-done.1
  93.6 4.0 %project.2.rest_0_ = f32[1024,128]{1,0:T(8,128)} custom-call(s32[1]{0:T(128)} %bitcast.13.side_ref, bf16[1024,4096]{1,0:T(8,128)(2,1)} %get-tuple-element.5.centered_ref, f32[2048,128]{1,0:T(8,128)} %copy-done.1), custom_call_target="tpu_custom_call" | custom-call | flops 536870912 | bytes 4194304 | tf_op jit(solution)/shard_map/project/pallas_call | solution.py:260
  97.6 0.0 collective-permute-done.4.basis_ref
  97.7 0.0 copy-start.3
  97.7 1.0 copy-done.3
  98.6 0.0 copy-start.2
  98.6 4.2 %project.3 = f32[1024,128]{1,0:T(8,128)} custom-call(s32[1]{0:T(128)} %bitcast.12.side_ref, bf16[1024,4096]{1,0:T(8,128)(2,1)} %get-tuple-element.5.centered_ref, f32[2048,128]{1,0:T(8,128)} %copy-done.3, f32[1024,128]{1,0:T(8,128)} %project.2.rest_0_), custom_call_target="tpu_custom_call" | custom-call | flops 536870912 | bytes 4194304 | tf_op jit(solution)/shard_map/project/pallas_call | solution.py:260
  102.9 17.4 %score_sum.1 = f32[128,128]{1,0:T(8,128)} custom-call(f32[8,128,128]{2,1,0:T(8,128)} %bitcast.38), custom_call_target="tpu_custom_call" | custom-call | tf_op jit(solution)/shard_map/score_sum/pallas_call | solution.py:113
  120.3 0.0 copy-done.2
  120.3 1.4 %select_bitcast_fusion.1 = (f32[1,2048,128]{2,1,0:T(8,128)S(1)}, f32[1,2048,128]{2,1,0:T(8,128)S(1)}) fusion(f32[2048,128]{1,0:T(8,128)} %copy-done.3, f32[2048,128]{1,0:T(8,128)S(1)} %copy-done.2, pred[]{:T(512)S(6)} %eq.7), kind=kLoop, calls=%fused_computation.6 | loop fusion | flops 524288 | bytes 4194305 | tf_op jit(solution)/shard_map/concatenate | solution.py:322
  121.7 0.0 copy-start.4
  121.7 1.5 %maximum_multiply_fusion = f32[1,4096,128]{2,1,0:T(8,128)} fusion(f32[1,2048,128]{2,1,0:T(8,128)S(1)} %get-tuple-element.7, f32[1,2048,128]{2,1,0:T(8,128)S(1)} %get-tuple-element.6), kind=kLoop, calls=%fused_computation.2 | loop fusion | flops 1048576 | bytes 4194304 | tf_op jit(solution)/shard_map/mul | solution.py:327
  123.2 0.0 copy-done.4
  123.2 0.6 copy.6
  (1 shorter events, 0.0 us)
Async XLA Ops:
  11.3 2.5 %copy-start = (f32[4096,128]{1,0:T(8,128)S(1)}, f32[4096,128]{1,0:T(8,128)}, u32[]{:S(2)}) copy-start(f32[4096,128]{1,0:T(8,128)} %get-tuple-element.4) | copy-start | bytes 6291460
  13.8 25.8 %collective-permute-start = (f32[2048,128]{1,0:T(8,128)}, f32[2048,128]{1,0:T(8,128)S(1)}, u32[]{:S(2)}, u32[]{:S(2)}) collective-permute-start(f32[2048,128]{1,0:T(8,128)} %constant_dynamic-slice_fusion), channel_id=1, source_target_pairs={{0,1},{1,0},{2,3},{3,2},{4,5},{5,4},{6,7},{7,6},{8,9},{9,8},{10,11... | collective-permute-start | bytes 3145736 | tf_op jit(solution)/shard_map/ppermute | solution.py:296
  13.8 17.2 %copy-start.5 = (f32[2,2,128,128]{3,2,1,0:T(8,128)S(1)}, f32[2,2,128,128]{3,2,1,0:T(8,128)}, u32[]{:S(2)}) copy-start(f32[2,2,128,128]{3,2,1,0:T(8,128)} %param.5) | copy-start | bytes 786436
  37.8 1.8 %collective-permute-start.1 = (f32[128,128]{1,0:T(8,128)}, f32[128,128]{1,0:T(8,128)S(1)}, u32[]{:S(2)}, u32[]{:S(2)}) collective-permute-start(f32[128,128]{1,0:T(8,128)} %mixing_map.2), channel_id=1, source_target_pairs={{0,1},{1,0},{2,3},{3,2},{4,5},{5,4},{6,7},{7,6},{8,9},{9,8},{10,11... | collective-permute-start | bytes 196616 | tf_op jit(solution)/shard_map/ppermute | solution.py:296
  40.6 27.6 %collective-permute-start.2 = (f32[2048,128]{1,0:T(8,128)S(1)}, f32[2048,128]{1,0:T(8,128)S(1)}, u32[]{:S(2)}, u32[]{:S(2)}) collective-permute-start(f32[2048,128]{1,0:T(8,128)S(1)} %convolution_add_fusion.1), channel_id=1, source_target_pairs={{0,2},{1,3},{2,0},{3,1},{4,6},{5,7},{6,4},{7,5},{8,10},{9,11},{10,... | collective-permute-start | bytes 3145736 | tf_op jit(solution)/shard_map/ppermute | solution.py:296
  63.7 4.5 %collective-permute-start.3 = (f32[128,128]{1,0:T(8,128)}, f32[128,128]{1,0:T(8,128)S(1)}, u32[]{:S(2)}, u32[]{:S(2)}) collective-permute-start(f32[128,128]{1,0:T(8,128)} %mixing_map.3), channel_id=1, source_target_pairs={{0,2},{1,3},{2,0},{3,1},{4,6},{5,7},{6,4},{7,5},{8,10},{9,11},{10,... | collective-permute-start | bytes 196616 | tf_op jit(solution)/shard_map/ppermute | solution.py:296
  92.6 1.1 copy-start.1
  92.6 5.1 %collective-permute-start.4 = (f32[2048,128]{1,0:T(8,128)S(1)}, f32[2048,128]{1,0:T(8,128)S(1)}, u32[]{:S(2)}, u32[]{:S(2)}) collective-permute-start(f32[2048,128]{1,0:T(8,128)S(1)} %fusion.6.basis_ref), channel_id=1, source_target_pairs={{0,1},{1,0},{2,3},{3,2},{4,5},{5,4},{6,7},{7,6},{8,9},{9,8},{10,11... | collective-permute-start | bytes 3145736 | tf_op jit(solution)/shard_map/ppermute | solution.py:296
  97.7 1.0 copy-start.3
  98.6 21.7 %copy-start.2 = (f32[2048,128]{1,0:T(8,128)S(1)}, f32[2048,128]{1,0:T(8,128)}, u32[]{:S(2)}) copy-start(f32[2048,128]{1,0:T(8,128)} %copy-done.1) | copy-start | bytes 3145732
  121.7 1.5 %copy-start.4 = (f32[128,128]{1,0:T(8,128)S(1)}, f32[128,128]{1,0:T(8,128)}, u32[]{:S(2)}) copy-start(f32[128,128]{1,0:T(8,128)} %score_sum.1) | copy-start | bytes 196612
where the time goes:
time: 125 us; the launch traced here: 124 us
  Pallas kernels  93.1 us (74%)
  matrix products  16.4 us (13%)
  local copies, waits for them, and re-layouts  6.3 us (5%)
  other arithmetic  2.87 us (2%)
  starting transfers between devices  2.29 us (2%)
  waiting for transfers between devices  2.1 us (2%)
    pallas_call x3, Pallas kernels, all_sum(): pl.pallas_call(functools.partial(all_sum_kernel, n, pair), out_shape=jax....  38.7 us
    pallas_call x1, Pallas kernels, score_sum(): pl.pallas_call(functools.partial(score_kernel, n, scale), out_shape=jax.S...  17.4 us
    pallas_call x2, Pallas kernels, mixing_map(): pl.pallas_call(map_kernel, out_shape=jax.ShapeDtypeStruct(gram.shape, gra...  12.2 us
    pallas_call x1, Pallas kernels, center_and_sketch(): pl.pallas_call(sketch_kernel, grid=(coords // tile,), out_shape=(jax.Shap...  10.6 us
    dot_general x3, matrix products, gram_of(): lax.dot_general(rows, rows, (((0,), (0,)), ((), ())), precision=HIGHEST)  9 us
    pallas_call x2, Pallas kernels, project(): pl.pallas_call(project_kernel, grid_spec=pltpu.PrefetchScalarGridSpec(num...  8.23 us
    pallas_call x1, Pallas kernels, lower_inverse(): pl.pallas_call(inverse_of, out_shape=jax.ShapeDtypeStruct(gram.shape, gra...  5.89 us
    dot_general x2, matrix products, mix(): jnp.matmul(own, own_map, precision=HIGHEST)  3.65 us
  transfers between devices with their start and end apart: 5, of which 1 were waited for; matrix products, arithmetic and copies ran while one was open for 9% of the time, Pallas kernels for 34%

commit v1 on v0

v1 whole, which is shorter than its diff:
```python
import functools
import math

import jax
import jax.numpy as jnp
from jax import lax
from jax.experimental import pallas as pl
from jax.experimental.pallas import tpu as pltpu
from jax.sharding import PartitionSpec as P

LEVELS = 2
HIGHEST = lax.Precision.HIGHEST
MESH = pl.DeviceIdType.MESH
VMEM = pl.BlockSpec(memory_space=pltpu.VMEM)


def peers_of(n, pair):
    coord = lax.axis_index("coord")
    if not pair:
        return coord, n, lambda rank: {"coord": rank}
    cohort = lax.axis_index("cohort")
    side = lax.rem(cohort, 2)
    base = cohort - side
    rank = coord * 2 + side
    return rank, 2 * n, lambda r: {"coord": r // 2, "cohort": base + lax.rem(r, 2)}


def greet(me, size, ident):
    barrier = pltpu.get_barrier_semaphore()
    for d in range(1, size):
        pl.semaphore_signal(
            barrier, inc=1, device_id=ident(lax.rem(me + d, size)), device_id_type=MESH
        )
    return barrier


def send_block(part_ref, recv, me, size, ident, send, got, d):
    peer = lax.rem(me + d, size)
    return pltpu.make_async_remote_copy(
        src_ref=part_ref.at[peer],
        dst_ref=recv.at[d],
        send_sem=send.at[d],
        recv_sem=got.at[d],
        device_id=ident(peer),
        device_id_type=MESH,
    )


def gram_sum_kernel(n, pair, count, *refs):
    rows_refs, (out_ref, gram, part, recv, send, got, send2, got2) = refs[:count], refs[count:]
    me, size, ident = peers_of(n, pair)
    barrier = greet(me, size, ident)
    block = part.shape[1]
    gram[...] = jnp.zeros_like(gram)
    for rows_ref in rows_refs:
        step = math.gcd(rows_ref.shape[0], 512)

        def add(i, carry, rows_ref=rows_ref, step=step):
            rows = rows_ref[pl.ds(pl.multiple_of(i * step, step), step), :]
            gram[...] += lax.dot_general(
                rows,
                rows,
                (((0,), (0,)), ((), ())),
                precision=HIGHEST,
                preferred_element_type=jnp.float32,
            )
            return carry

        lax.fori_loop(0, rows_ref.shape[0] // step, add, 0)
    for r in range(size):
        part[r] = gram[r * block : (r + 1) * block, :]
    pl.semaphore_wait(barrier, size - 1)
    copies = [send_block(part, recv, me, size, ident, send, got, d) for d in range(1, size)]
    for copy in copies:
        copy.start()
    total = part[me]
    for d in range(1, size):
        copies[d - 1].wait_recv()
        total = total + recv[d]
    out_ref[me] = total
    spread = []
    for d in range(1, size):
        spread.append(
            pltpu.make_async_remote_copy(
                src_ref=out_ref.at[me],
                dst_ref=out_ref.at[me],
                send_sem=send2.at[d],
                recv_sem=got2.at[d],
                device_id=ident(lax.rem(me + d, size)),
                device_id_type=MESH,
            )
        )
    for copy in spread:
        copy.start()
    for copy in spread:
        copy.wait_recv()
    for copy in copies + spread:
        copy.wait_send()


def gram_sum(parts, n, pair, ident):
    size = 2 * n if pair else n
    width = parts[0].shape[1]
    dtype = parts[0].dtype
    shape = (size, width // size, width)
    out = pl.pallas_call(
        functools.partial(gram_sum_kernel, n, pair, len(parts)),
        out_shape=jax.ShapeDtypeStruct(shape, dtype),
        in_specs=[VMEM] * len(parts),
        out_specs=VMEM,
        scratch_shapes=[
            pltpu.VMEM((width, width), dtype),
            pltpu.VMEM(shape, dtype),
            pltpu.VMEM(shape, dtype),
        ]
        + [pltpu.SemaphoreType.DMA((size,))] * 4,
        compiler_params=pltpu.CompilerParams(collective_id=ident, has_side_effects=True),
        name=f"gram_sum_{ident}",
    )(*parts)
    return out.reshape(width, width)


def score_kernel(
    n, scale, centered_ref, own_ref, basis_ref, out_ref,
    held, narrow, part, recv, loaded, send, got, swap_send, swap_got,
):
    me, size, ident = peers_of(n, False)
    cohort = lax.axis_index("cohort")
    side = lax.rem(cohort, 2)
    partner = {"cohort": cohort + 1 - 2 * side}
    rows, half = held.shape[2:]
    order = [lax.rem(me + d, size) for d in list(range(1, size)) + [0]]
    loads = []
    for peer in order:
        pair = []
        for h in range(2):
            pair.append(
                pltpu.make_async_copy(
                    centered_ref.at[
                        pl.ds(pl.multiple_of(peer * rows, rows), rows), pl.ds(h * half, half)
                    ],
                    held.at[peer, h],
                    loaded.at[peer, h],
                )
            )
        loads.append(pair)
        for copy in pair:
            copy.start()
    barrier = greet(me, size, ident)
    pl.semaphore_signal(barrier, inc=1, device_id=partner, device_id_type=MESH)
    basis_ref[side] = own_ref[...]
    narrow[...] = own_ref[...].astype(jnp.bfloat16)
    pl.semaphore_wait(barrier, size)
    cross = pltpu.make_async_remote_copy(
        src_ref=own_ref,
        dst_ref=basis_ref.at[side],
        send_sem=swap_send,
        recv_sem=swap_got,
        device_id=partner,
        device_id_type=MESH,
    )
    cross.start()
    for peer, pair in zip(order, loads):
        for copy in pair:
            copy.wait()
        part[peer] = jnp.dot(held[peer, side], narrow[...], preferred_element_type=jnp.float32)
    cross.wait_recv()
    narrow[...] = basis_ref[1 - side].astype(jnp.bfloat16)
    copies = []
    for d, peer in zip(list(range(1, size)) + [0], order):
        part[peer] = part[peer] + jnp.dot(
            held[peer, 1 - side], narrow[...], preferred_element_type=jnp.float32
        )
        if d:
            copies.append(send_block(part, recv, me, size, ident, send, got, d))
            copies[-1].start()
    total = part[me]
    for d in range(1, size):
        copies[d - 1].wait_recv()
        total = total + recv[d]
    out_ref[...] = total * scale
    cross.wait_send()
    for copy in copies:
        copy.wait_send()


def basis_and_scores(centered, own, n, scale, ident):
    subjects = centered.shape[0]
    half, width = own.shape
    rows = subjects // n
    blocks = (n, rows, width)
    basis, scores = pl.pallas_call(
        functools.partial(score_kernel, n, scale),
        out_shape=(
            jax.ShapeDtypeStruct((2, half, width), own.dtype),
            jax.ShapeDtypeStruct((rows, width), jnp.float32),
        ),
        in_specs=[pl.BlockSpec(memory_space=pl.ANY), VMEM],
        out_specs=(VMEM, VMEM),
        scratch_shapes=[
            pltpu.VMEM((n, 2, rows, half), centered.dtype),
            pltpu.VMEM((half, width), jnp.bfloat16),
            pltpu.VMEM(blocks, jnp.float32),
            pltpu.VMEM(blocks, jnp.float32),
            pltpu.SemaphoreType.DMA((n, 2)),
            pltpu.SemaphoreType.DMA((n,)),
            pltpu.SemaphoreType.DMA((n,)),
            pltpu.SemaphoreType.DMA,
            pltpu.SemaphoreType.DMA,
        ],
        compiler_params=pltpu.CompilerParams(collective_id=ident, has_side_effects=True),
        name="basis_and_scores",
    )(centered, own)
    return basis.reshape(2 * half, width), scores


def inverse_of(g_ref, x_ref):
    size = g_ref.shape[0]
    step = 8
    tiles = size // step
    lane = lax.broadcasted_iota(jnp.int32, (step, size), 1)
    sub = lax.broadcasted_iota(jnp.int32, (step, size), 0)

    def full(x):
        return jnp.broadcast_to(x, (step, size))

    def total(terms):
        while len(terms) > 1:
            terms = [terms[i] + terms[i + 1] for i in range(0, len(terms), 2)]
        return terms[0]

    left = [g_ref[t * step : (t + 1) * step, :] for t in range(tiles)]
    right = [(lane == sub + t * step).astype(jnp.float32) for t in range(tiles)]
    for t in range(tiles):
        at = t * step
        cols = [full(left[t][:, at + k : at + k + 1]) for k in range(step)]
        e = [[full(cols[k][i : i + 1, :]) for k in range(i + 1)] for i in range(step)]
        rows = [full(left[t][i : i + 1, :]) for i in range(step)]
        rows_x = [full(right[t][i : i + 1, :]) for i in range(step)]
        f = {}
        inv = []
        for s in range(step):
            inv.append(1.0 / e[s][s])
            for i in range(s + 1, step):
                f[i, s] = e[i][s] * inv[s]
                for k in range(s + 1, i + 1):
                    e[i][k] = e[i][k] - f[i, s] * e[k][s]
            for i in range(s + 1, step):
                rows[i] = rows[i] - f[i, s] * rows[s]
                rows_x[i] = rows_x[i] - f[i, s] * rows_x[s]
        out = rows_x[0] * lax.rsqrt(e[0][0])
        for s in range(1, step):
            out = jnp.where(sub == s, rows_x[s] * lax.rsqrt(e[s][s]), out)
        x_ref[at : at + step, :] = out
        rows = [rows[s] * inv[s] for s in range(step)]
        rows_x = [rows_x[s] * inv[s] for s in range(step)]
        for u in range(t + 1, tiles):
            c = [full(left[u][:, at + s : at + s + 1]) for s in range(step)]
            for s in range(step):
                for r in range(s):
                    c[s] = c[s] - f[s, r] * c[r]
            left[u] = left[u] - total([c[s] * rows[s] for s in range(step)])
            right[u] = right[u] - total([c[s] * rows_x[s] for s in range(step)])


def map_kernel(g_ref, mix_ref, out_ref, x_ref):
    inverse_of(g_ref, x_ref)
    out_ref[...] = lax.dot_general(
        x_ref[...],
        mix_ref[...],
        (((0,), (0,)), ((), ())),
        precision=HIGHEST,
        preferred_element_type=jnp.float32,
    )


def lower_inverse(gram):
    return pl.pallas_call(
        inverse_of,
        out_shape=jax.ShapeDtypeStruct(gram.shape, gram.dtype),
        in_specs=[VMEM],
        out_specs=VMEM,
        name="lower_inverse",
    )(gram)


def mixing_map(gram, mix):
    return pl.pallas_call(
        map_kernel,
        out_shape=jax.ShapeDtypeStruct(gram.shape, gram.dtype),
        in_specs=[VMEM, VMEM],
        out_specs=VMEM,
        scratch_shapes=[pltpu.VMEM(gram.shape, gram.dtype)],
        name="mixing_map",
    )(gram, mix)


def sketch_kernel(steps, side_ref, shapes_ref, signs_ref, centered_ref, mine_ref, given_ref, turned):
    i = pl.program_id(0)

    @pl.when(i == 0)
    def _():
        turned[...] = signs_ref[...].astype(jnp.float32).T.astype(jnp.bfloat16)

    data = shapes_ref[...].astype(jnp.float32)
    mean = jnp.sum(data, axis=0, keepdims=True) * (1.0 / data.shape[0])
    centered = (data - mean).astype(jnp.bfloat16)
    centered_ref[...] = centered
    sketch = jnp.dot(turned[...], centered, preferred_element_type=jnp.float32).T

    @pl.when(i < steps)
    def _():
        mine_ref[...] = sketch

    @pl.when(i >= steps)
    def _():
        given_ref[...] = sketch


def center_and_sketch(side, shapes, signs):
    subjects, coords = shapes.shape
    width = signs.shape[1]
    half = coords // 2
    tile = math.gcd(half, 512)
    steps = half // tile

    def column(i, side):
        kept = i < steps
        return jnp.where(kept, side[0] * steps + i, (1 - side[0]) * steps + i - steps)

    return pl.pallas_call(
        functools.partial(sketch_kernel, steps),
        grid_spec=pltpu.PrefetchScalarGridSpec(
            num_scalar_prefetch=1,
            grid=(2 * steps,),
            in_specs=[
                pl.BlockSpec((subjects, tile), lambda i, side: (0, column(i, side))),
                pl.BlockSpec((subjects, width), lambda i, side: (0, 0)),
            ],
            out_specs=(
                pl.BlockSpec((subjects, tile), lambda i, side: (0, column(i, side))),
                pl.BlockSpec((tile, width), lambda i, side: (jnp.minimum(i, steps - 1), 0)),
                pl.BlockSpec((tile, width), lambda i, side: (jnp.maximum(i - steps, 0), 0)),
            ),
            scratch_shapes=[pltpu.VMEM((width, subjects), jnp.bfloat16)],
        ),
        out_shape=(
            jax.ShapeDtypeStruct((subjects, coords), jnp.bfloat16),
            jax.ShapeDtypeStruct((half, width), jnp.float32),
            jax.ShapeDtypeStruct((half, width), jnp.float32),
        ),
        name="center_and_sketch",
    )(side.reshape(1), shapes, signs)


def times_t(a, b):
    return lax.dot_general(a, b, (((1,), (1,)), ((), ())), precision=HIGHEST)


def mix(own, own_map, other, other_map):
    return jnp.matmul(own, own_map, precision=HIGHEST) + jnp.matmul(
        other, other_map, precision=HIGHEST
    )


def swap(value, distance):
    size = lax.axis_size("cohort")
    return lax.ppermute(value, "cohort", [(i, i ^ distance) for i in range(size)])


def on_device(shapes, sketch_signs, merge_sketch):
    n = lax.axis_size("coord")
    position = lax.axis_index("cohort")
    side = position % 2
    upper = position // 2 % 2
    centered, mine, given = center_and_sketch(side, shapes[0], sketch_signs[0])

    theirs = swap(given, 1)
    own_map = mixing_map(gram_sum((mine, given), n, False, 0), merge_sketch[0][side])
    mine = mix(mine, own_map, theirs, swap(own_map, 1))

    theirs = swap(mine, 2)
    own_map = mixing_map(gram_sum((mine,), n, True, 1), merge_sketch[1][upper])
    mine = mix(mine, own_map, theirs, swap(own_map, 2))

    mine = times_t(mine, lower_inverse(gram_sum((mine,), n, True, 2)))
    width = mine.shape[1]
    total_coords = shapes.shape[2] * n
    basis, scores = basis_and_scores(
        centered, mine, n, 4.0 * math.sqrt(width / total_coords), 3
    )
    return (basis * math.sqrt(total_coords))[None], scores[None]


def solution(mesh):
    placed = (P("cohort", None, "coord"), P("cohort", None, None), P())
    return jax.shard_map(
        on_device,
        mesh=mesh,
        in_specs=placed,
        out_specs=(P("cohort", "coord", None), P("cohort", "coord", None)),
        check_vma=False,
    )
```

time: 125 us -> 115 us (0.920)
  matrix products: 16.4 us -> 10.1 us
  local copies, waits for them, and re-layouts: 6.3 us -> 1.94 us
    dot_general x3 -> x0, matrix products: 9 us -> none  [gram_of(): lax.dot_general(rows, rows, (((0,), (0,)), ((), ())), precision=HIGHEST)]
    dynamic_slice x1 -> x0, local copies, waits for them, and re-layouts: 2.51 us -> none  [on_device(): lax.dynamic_slice_in_dim(sketch, (1 - side) * half, half, 0)]
    unnamed x13 -> x9, local copies, waits for them, and re-layouts: 2.5 us -> 0.65 us
    mul x1, other arithmetic: 1.5 us -> 3.12 us  [on_device(): return ((basis * math.sqrt(total_coords))[None], scores[None])]
    dot_general x1, matrix products: 1.82 us -> 3.2 us  [times_t(): return lax.dot_general(a, b, (((1,), (1,)), ((), ())), precision=HIGHEST)]
    concatenate x1 -> x0, other arithmetic: 1.36 us -> none  [on_device(): current = jnp.concatenate([first, second], axis=0)]
    pallas_call x7 -> x5, Pallas kernels: 75 us -> 76 us  [the longest x3 41.7 us: gram_sum(): pl.pallas_call(functools.partial(gram_sum_kernel, n, pair, len(parts)), o...]
  transfers between devices with their start and end apart: 5 -> 4, of which waited for: 1 -> 1; matrix products, arithmetic and copies ran while one was open for 9% -> 5% of each run, Pallas kernels for 34% -> 35%
where the time goes in v1:
time: 115 us; the launch traced here: 114 us
  Pallas kernels  93.9 us (82%)
  matrix products  10.1 us (9%)
  other arithmetic  3.12 us (3%)
  waiting for transfers between devices  2.42 us (2%)
  starting transfers between devices  2.15 us (2%)
  local copies, waits for them, and re-layouts  1.94 us (2%)
    pallas_call x3, Pallas kernels, gram_sum(): pl.pallas_call(functools.partial(gram_sum_kernel, n, pair, len(parts)), o...  41.7 us
    pallas_call x1, Pallas kernels, basis_and_scores(): pl.pallas_call(functools.partial(score_kernel, n, scale), out_shape=(jax....  22.6 us
    pallas_call x2, Pallas kernels, mixing_map(): pl.pallas_call(map_kernel, out_shape=jax.ShapeDtypeStruct(gram.shape, gra...  12.2 us
    pallas_call x1, Pallas kernels, center_and_sketch(): pl.pallas_call(functools.partial(sketch_kernel, steps), grid_spec=pltpu.P...  11.7 us
    pallas_call x1, Pallas kernels, lower_inverse(): pl.pallas_call(inverse_of, out_shape=jax.ShapeDtypeStruct(gram.shape, gra...  5.68 us
    dot_general x2, matrix products, mix(): jnp.matmul(own, own_map, precision=HIGHEST)  4 us
    dot_general x1, matrix products, times_t(): return lax.dot_general(a, b, (((1,), (1,)), ((), ())), precision=HIGHEST)  3.2 us
    mul x1, other arithmetic, on_device(): return ((basis * math.sqrt(total_coords))[None], scores[None])  3.12 us
  transfers between devices with their start and end apart: 4, of which 1 were waited for; matrix products, arithmetic and copies ran while one was open for 5% of the time, Pallas kernels for 35%

profile of v1, /device:TPU:12, one launch (start us, length us, event | category | flops | bytes accessed | tf_op | source)
XLA Modules:
  0.0 114.4 jit_solution(2821868922596190403)
XLA Ops:
  0.6 11.7 %center_and_sketch.1 = (bf16[1024,4096]{1,0:T(8,128)(2,1)}, f32[2048,128]{1,0:T(8,128)}, f32[2048,128]{1,0:T(8,128)}) custom-call(s32[1]{0:T(128)} %bitcast.side_ref, bf16[1024,4096]{1,0:T(8,128)(2,1)} %bitcast.22, s32[1024,128]{1,0:T(8,128)} %bitcast.24), custom_call_target="tpu_custom_call" | custom-call | tf_op jit(solution)/shard_map/center_and_sketch/pallas_call | solution.py:331
  12.4 0.0 copy-start.2
  12.4 0.0 copy-start.1
  12.4 0.1 collective-permute-start
  12.5 14.5 %gram_sum_0.1 = f32[8,16,128]{2,1,0:T(8,128)} custom-call(f32[2048,128]{1,0:T(8,128)} %get-tuple-element.8.refs_0_, f32[2048,128]{1,0:T(8,128)} %get-tuple-element.9.refs_1_), custom_call_target="tpu_custom_call" | custom-call | tf_op jit(solution)/shard_map/gram_sum_0/pallas_call | solution.py:106
  27.0 0.0 copy-done.2
  27.0 0.6 dynamic-slice_bitcast_fusion.1.mix_ref
  27.7 6.1 %mixing_map.2 = f32[128,128]{1,0:T(8,128)} custom-call(f32[128,128]{1,0:T(8,128)} %bitcast.25, f32[128,128]{1,0:T(8,128)} %dynamic-slice_bitcast_fusion.1.mix_ref), custom_call_target="tpu_custom_call" | custom-call | tf_op jit(solution)/shard_map/mixing_map/pallas_call | solution.py:288
  33.8 0.0 collective-permute-start.1
  33.8 0.0 copy-done.1
  33.8 1.8 %fusion.1 = f32[2048,128]{1,0:T(8,128)S(1)} fusion(f32[2048,128]{1,0:T(8,128)S(1)} %copy-done.1, f32[128,128]{1,0:T(8,128)} %mixing_map.2), kind=kOutput, calls=%fused_computation.6 | convolution fusion | flops 402653184 | bytes 2162688 | tf_op jit(solution)/shard_map/dot_general | solution.py:361
  35.6 0.0 collective-permute-done.1
  35.6 0.0 collective-permute-done
  35.6 1.0 convolution_add_fusion.1.refs_0_
  36.6 0.0 copy-start
  36.6 1.6 %collective-permute-start.2 = (f32[2048,128]{1,0:T(8,128)S(1)}, f32[2048,128]{1,0:T(8,128)S(1)}, u32[]{:S(2)}, u32[]{:S(2)}) collective-permute-start(f32[2048,128]{1,0:T(8,128)S(1)} %convolution_add_fusion.1.refs_0_), channel_id=1, source_target_pairs={{0,2},{1,3},{2,0},{3,1},{4,6},{5,7},{6,4},{7,5},{8,10},{9,11},{10,... | collective-permute-start | bytes 3145736 | tf_op jit(solution)/shard_map/ppermute | solution.py:368
  38.1 0.6 dynamic-slice_bitcast_fusion.mix_ref
  38.8 0.0 copy-done
  38.8 13.6 %gram_sum_1.1 = f32[16,8,128]{2,1,0:T(8,128)} custom-call(f32[2048,128]{1,0:T(8,128)} %copy-done), custom_call_target="tpu_custom_call" | custom-call | tf_op jit(solution)/shard_map/gram_sum_1/pallas_call | solution.py:106
  52.4 6.1 %mixing_map.3 = f32[128,128]{1,0:T(8,128)} custom-call(f32[128,128]{1,0:T(8,128)} %bitcast.26, f32[128,128]{1,0:T(8,128)} %dynamic-slice_bitcast_fusion.mix_ref), custom_call_target="tpu_custom_call" | custom-call | tf_op jit(solution)/shard_map/mixing_map/pallas_call | solution.py:288
  58.5 0.5 collective-permute-start.3
  59.0 2.2 %fusion.2 = f32[2048,128]{1,0:T(8,128)S(1)} fusion(f32[2048,128]{1,0:T(8,128)} %copy-done, f32[128,128]{1,0:T(8,128)} %mixing_map.3), kind=kOutput, calls=%fused_computation.7 | convolution fusion | flops 402653184 | bytes 2162688 | tf_op jit(solution)/shard_map/dot_general | solution.py:361
  61.2 2.4 %collective-permute-done.3 = f32[128,128]{1,0:T(8,128)S(1)} collective-permute-done((f32[128,128]{1,0:T(8,128)}, f32[128,128]{1,0:T(8,128)S(1)}, u32[]{:S(2)}, u32[]{:S(2)}) %collective-permute-start.3) | collective-permute-done | bytes 65568 | tf_op jit(solution)/shard_map/ppermute | solution.py:368
  63.6 0.0 collective-permute-done.2
  63.6 1.9 %convolution_add_fusion.refs_0_ = f32[2048,128]{1,0:T(8,128)} fusion(f32[2048,128]{1,0:T(8,128)S(1)} %fusion.2, f32[2048,128]{1,0:T(8,128)S(1)} %collective-permute-done.2, f32[128,128]{1,0:T(8,128)S(1)} %collective-permute-done.3), kind=kOutput, calls=%fused_computation | convolution fusion | flops 402915328 | bytes 3211264 | tf_op jit(solution)/shard_map/dot_general | solution.py:361
  65.6 13.6 %gram_sum_2.1 = f32[16,8,128]{2,1,0:T(8,128)} custom-call(f32[2048,128]{1,0:T(8,128)} %convolution_add_fusion.refs_0_), custom_call_target="tpu_custom_call" | custom-call | tf_op jit(solution)/shard_map/gram_sum_2/pallas_call | solution.py:106
  79.2 5.7 %lower_inverse.1 = f32[128,128]{1,0:T(8,128)} custom-call(f32[128,128]{1,0:T(8,128)} %bitcast.27), custom_call_target="tpu_custom_call" | custom-call | tf_op jit(solution)/shard_map/lower_inverse/pallas_call | solution.py:278
  84.9 3.2 %fusion.3.own_ref = f32[2048,128]{1,0:T(8,128)} fusion(f32[2048,128]{1,0:T(8,128)} %convolution_add_fusion.refs_0_, f32[128,128]{1,0:T(8,128)} %lower_inverse.1), kind=kOutput, calls=%fused_computation.8 | convolution fusion | flops 402653184 | bytes 2162688 | tf_op jit(solution)/shard_map/dot_general | solution.py:357
  88.1 22.6 %basis_and_scores.1 = (f32[2,2048,128]{2,1,0:T(8,128)}, f32[128,128]{1,0:T(8,128)}) custom-call(bf16[1024,4096]{1,0:T(8,128)(2,1)} %get-tuple-element.7.centered_ref, f32[2048,128]{1,0:T(8,128)} %fusion.3.own_ref), custom_call_target="tpu_custom_call" | custom-call | tf_op jit(solution)/shard_map/basis_and_scores/pallas_call | solution.py:192
  110.6 0.0 copy-start.3
  110.7 3.1 %broadcast_multiply_fusion = f32[2,2048,128]{2,1,0:T(8,128)} fusion(f32[2,2048,128]{2,1,0:T(8,128)} %get-tuple-element.10), kind=kLoop, calls=%fused_computation.2 | loop fusion | flops 524288 | bytes 4194304 | tf_op jit(solution)/shard_map/mul | solution.py:392
  113.8 0.0 copy-done.3
  113.8 0.6 copy.6
  (1 shorter events, 0.0 us)
Async XLA Ops:
  12.4 14.6 %copy-start.2 = (f32[2,2,128,128]{3,2,1,0:T(8,128)S(1)}, f32[2,2,128,128]{3,2,1,0:T(8,128)}, u32[]{:S(2)}) copy-start(f32[2,2,128,128]{3,2,1,0:T(8,128)} %param.5) | copy-start | bytes 786436
  12.4 21.4 %copy-start.1 = (f32[2048,128]{1,0:T(8,128)S(1)}, f32[2048,128]{1,0:T(8,128)}, u32[]{:S(2)}) copy-start(f32[2048,128]{1,0:T(8,128)} %get-tuple-element.8.refs_0_) | copy-start | bytes 3145732
  12.4 23.2 %collective-permute-start = (f32[2048,128]{1,0:T(8,128)}, f32[2048,128]{1,0:T(8,128)S(1)}, u32[]{:S(2)}, u32[]{:S(2)}) collective-permute-start(f32[2048,128]{1,0:T(8,128)} %get-tuple-element.9.refs_1_), channel_id=1, source_target_pairs={{0,1},{1,0},{2,3},{3,2},{4,5},{5,4},{6,7},{7,6},{8,9},{9,8},{10,11... | collective-permute-start | bytes 3145736 | tf_op jit(solution)/shard_map/ppermute | solution.py:368
  33.8 1.8 %collective-permute-start.1 = (f32[128,128]{1,0:T(8,128)}, f32[128,128]{1,0:T(8,128)S(1)}, u32[]{:S(2)}, u32[]{:S(2)}) collective-permute-start(f32[128,128]{1,0:T(8,128)} %mixing_map.2), channel_id=1, source_target_pairs={{0,1},{1,0},{2,3},{3,2},{4,5},{5,4},{6,7},{7,6},{8,9},{9,8},{10,11... | collective-permute-start | bytes 196616 | tf_op jit(solution)/shard_map/ppermute | solution.py:368
  36.6 2.2 %copy-start = (f32[2048,128]{1,0:T(8,128)}, f32[2048,128]{1,0:T(8,128)S(1)}, u32[]{:S(2)}) copy-start(f32[2048,128]{1,0:T(8,128)S(1)} %convolution_add_fusion.1.refs_0_) | copy-start | bytes 3145732
  36.6 27.0 %collective-permute-start.2 = (f32[2048,128]{1,0:T(8,128)S(1)}, f32[2048,128]{1,0:T(8,128)S(1)}, u32[]{:S(2)}, u32[]{:S(2)}) collective-permute-start(f32[2048,128]{1,0:T(8,128)S(1)} %convolution_add_fusion.1.refs_0_), channel_id=1, source_target_pairs={{0,2},{1,3},{2,0},{3,1},{4,6},{5,7},{6,4},{7,5},{8,10},{9,11},{10,... | collective-permute-start | bytes 3145736 | tf_op jit(solution)/shard_map/ppermute | solution.py:368
  58.5 5.2 %collective-permute-start.3 = (f32[128,128]{1,0:T(8,128)}, f32[128,128]{1,0:T(8,128)S(1)}, u32[]{:S(2)}, u32[]{:S(2)}) collective-permute-start(f32[128,128]{1,0:T(8,128)} %mixing_map.3), channel_id=1, source_target_pairs={{0,2},{1,3},{2,0},{3,1},{4,6},{5,7},{6,4},{7,5},{8,10},{9,11},{10,... | collective-permute-start | bytes 196616 | tf_op jit(solution)/shard_map/ppermute | solution.py:368
  110.6 3.1 %copy-start.3 = (f32[128,128]{1,0:T(8,128)S(1)}, f32[128,128]{1,0:T(8,128)}, u32[]{:S(2)}) copy-start(f32[128,128]{1,0:T(8,128)} %get-tuple-element.11) | copy-start | bytes 196612

commit v2 on v1

--- a/solution.py
+++ b/solution.py
@@ -47,26 +47,36 @@
 
 
 def gram_sum_kernel(n, pair, count, *refs):
-    rows_refs, (out_ref, gram, part, recv, send, got, send2, got2) = refs[:count], refs[count:]
+    rows_refs, (out_ref, gram, cross, part, recv, send, got, send2, got2) = refs[:count], refs[count:]
     me, size, ident = peers_of(n, pair)
     barrier = greet(me, size, ident)
     block = part.shape[1]
+    width = gram.shape[0]
     gram[...] = jnp.zeros_like(gram)
+    cross[...] = jnp.zeros_like(cross)
+
+    def product(a, b):
+        return lax.dot_general(
+            a, b, (((0,), (0,)), ((), ())), preferred_element_type=jnp.float32
+        )
+
     for rows_ref in rows_refs:
         step = math.gcd(rows_ref.shape[0], 512)
 
         def add(i, carry, rows_ref=rows_ref, step=step):
             rows = rows_ref[pl.ds(pl.multiple_of(i * step, step), step), :]
-            gram[...] += lax.dot_general(
-                rows,
-                rows,
-                (((0,), (0,)), ((), ())),
-                precision=HIGHEST,
-                preferred_element_type=jnp.float32,
-            )
+            high = rows.astype(jnp.bfloat16)
+            rest = rows - high.astype(jnp.float32)
+            middle = rest.astype(jnp.bfloat16)
+            low = (rest - middle.astype(jnp.float32)).astype(jnp.bfloat16)
+            wide = product(high, jnp.concatenate([high, middle], axis=1))
+            gram[...] += wide[:, :width] + product(middle, middle)
+            cross[...] += wide[:, width:] + product(high, low)
             return carry
 
         lax.fori_loop(0, rows_ref.shape[0] // step, add, 0)
+    turned = cross[...]
+    gram[...] += turned + turned.T
     for r in range(size):
         part[r] = gram[r * block : (r + 1) * block, :]
     pl.semaphore_wait(barrier, size - 1)
@@ -110,6 +120,7 @@
         out_specs=VMEM,
         scratch_shapes=[
             pltpu.VMEM((width, width), dtype),
+            pltpu.VMEM((width, width), dtype),
             pltpu.VMEM(shape, dtype),
             pltpu.VMEM(shape, dtype),
         ]
@@ -121,7 +132,7 @@
 
 
 def score_kernel(
-    n, scale, centered_ref, own_ref, basis_ref, out_ref,
+    n, scale, grow, centered_ref, own_ref, basis_ref, out_ref,
     held, narrow, part, recv, loaded, send, got, swap_send, swap_got,
 ):
     me, size, ident = peers_of(n, False)
@@ -174,6 +185,7 @@
         if d:
             copies.append(send_block(part, recv, me, size, ident, send, got, d))
             copies[-1].start()
+    basis_ref[...] = basis_ref[...] * grow
     total = part[me]
     for d in range(1, size):
         copies[d - 1].wait_recv()
@@ -184,13 +196,13 @@
         copy.wait_send()
 
 
-def basis_and_scores(centered, own, n, scale, ident):
+def basis_and_scores(centered, own, n, scale, grow, ident):
     subjects = centered.shape[0]
     half, width = own.shape
     rows = subjects // n
     blocks = (n, rows, width)
     basis, scores = pl.pallas_call(
-        functools.partial(score_kernel, n, scale),
+        functools.partial(score_kernel, n, scale, grow),
         out_shape=(
             jax.ShapeDtypeStruct((2, half, width), own.dtype),
             jax.ShapeDtypeStruct((rows, width), jnp.float32),
@@ -321,7 +333,7 @@
     subjects, coords = shapes.shape
     width = signs.shape[1]
     half = coords // 2
-    tile = math.gcd(half, 512)
+    tile = math.gcd(half, 2048)
     steps = half // tile
 
     def column(i, side):
@@ -387,9 +399,9 @@
     width = mine.shape[1]
     total_coords = shapes.shape[2] * n
     basis, scores = basis_and_scores(
-        centered, mine, n, 4.0 * math.sqrt(width / total_coords), 3
-    )
-    return (basis * math.sqrt(total_coords))[None], scores[None]
+        centered, mine, n, 4.0 * math.sqrt(width / total_coords), math.sqrt(total_coords), 3
+    )
+    return basis[None], scores[None]
 
 
 def solution(mesh):

time: 115 us -> 113 us (0.983)
  local copies, waits for them, and re-layouts: 1.94 us -> 5.82 us
  Pallas kernels: 93.9 us -> 90.7 us
  other arithmetic: 3.12 us -> 0 us
    unnamed x9 -> x6, local copies, waits for them, and re-layouts: 0.65 us -> 4.53 us
    mul x1 -> x0, other arithmetic: 3.12 us -> none  [on_device(): return ((basis * math.sqrt(total_coords))[None], scores[None])]
    pallas_call x1, Pallas kernels: 11.7 us -> 9.63 us  [center_and_sketch(): pl.pallas_call(functools.partial(sketch_kernel, steps), grid_spec=pltpu.P...]
where the time goes in v2:
time: 113 us; the launch traced here: 112 us
  Pallas kernels  90.7 us (80%)
  matrix products  10.5 us (9%)
  local copies, waits for them, and re-layouts  5.82 us (5%)
  waiting for transfers between devices  2.6 us (2%)
  starting transfers between devices  2.1 us (2%)
    pallas_call x3, Pallas kernels, gram_sum(): pl.pallas_call(functools.partial(gram_sum_kernel, n, pair, len(parts)), o...  40.6 us
    pallas_call x1, Pallas kernels, basis_and_scores(): pl.pallas_call(functools.partial(score_kernel, n, scale, grow), out_shape...  22.6 us
    pallas_call x2, Pallas kernels, mixing_map(): pl.pallas_call(map_kernel, out_shape=jax.ShapeDtypeStruct(gram.shape, gra...  12.2 us
    pallas_call x1, Pallas kernels, center_and_sketch(): pl.pallas_call(functools.partial(sketch_kernel, steps), grid_spec=pltpu.P...  9.63 us
    pallas_call x1, Pallas kernels, lower_inverse(): pl.pallas_call(inverse_of, out_shape=jax.ShapeDtypeStruct(gram.shape, gra...  5.68 us
    unnamed x6, local copies, waits for them, and re-layouts  4.53 us
    dot_general x2, matrix products, mix(): jnp.matmul(own, own_map, precision=HIGHEST)  4.39 us
    dot_general x1, matrix products, times_t(): return lax.dot_general(a, b, (((1,), (1,)), ((), ())), precision=HIGHEST)  3.19 us
  transfers between devices with their start and end apart: 4, of which 1 were waited for; matrix products, arithmetic and copies ran while one was open for 5% of the time, Pallas kernels for 35%

profile of v2, /device:TPU:12, one launch (start us, length us, event | category | flops | bytes accessed | tf_op | source)
XLA Modules:
  0.0 112.5 jit_solution(494960051169775755)
XLA Ops:
  0.6 0.0 copy-start.1
  0.7 9.6 %center_and_sketch.1 = (bf16[1024,4096]{1,0:T(8,128)(2,1)}, f32[2048,128]{1,0:T(8,128)}, f32[2048,128]{1,0:T(8,128)}) custom-call(s32[1]{0:T(128)} %bitcast.side_ref, bf16[1024,4096]{1,0:T(8,128)(2,1)} %bitcast.22, s32[1024,128]{1,0:T(8,128)} %bitcast.24), custom_call_target="tpu_custom_call" | custom-call | tf_op jit(solution)/shard_map/center_and_sketch/pallas_call | solution.py:343
  10.3 0.0 collective-permute-start
  10.3 13.8 %gram_sum_0.1 = f32[8,16,128]{2,1,0:T(8,128)} custom-call(f32[2048,128]{1,0:T(8,128)} %get-tuple-element.8.refs_0_, f32[2048,128]{1,0:T(8,128)} %get-tuple-element.9.refs_1_), custom_call_target="tpu_custom_call" | custom-call | tf_op jit(solution)/shard_map/gram_sum_0/pallas_call | solution.py:116
  24.1 0.0 copy-done.1
  24.1 0.6 dynamic-slice_bitcast_fusion.1.mix_ref
  24.8 6.1 %mixing_map.2 = f32[128,128]{1,0:T(8,128)} custom-call(f32[128,128]{1,0:T(8,128)} %bitcast.25, f32[128,128]{1,0:T(8,128)} %dynamic-slice_bitcast_fusion.1.mix_ref), custom_call_target="tpu_custom_call" | custom-call | tf_op jit(solution)/shard_map/mixing_map/pallas_call | solution.py:300
  30.9 0.0 collective-permute-start.1
  30.9 2.2 %fusion.1 = f32[2048,128]{1,0:T(8,128)S(1)} fusion(f32[2048,128]{1,0:T(8,128)} %get-tuple-element.8.refs_0_, f32[128,128]{1,0:T(8,128)} %mixing_map.2), kind=kOutput, calls=%fused_computation.5 | convolution fusion | flops 402653184 | bytes 2162688 | tf_op jit(solution)/shard_map/dot_general | solution.py:373
  33.1 0.0 collective-permute-done.1
  33.1 0.0 collective-permute-done
  33.1 1.0 convolution_add_fusion.1.refs_0_
  34.1 0.0 copy-start
  34.1 1.6 %collective-permute-start.2 = (f32[2048,128]{1,0:T(8,128)S(1)}, f32[2048,128]{1,0:T(8,128)S(1)}, u32[]{:S(2)}, u32[]{:S(2)}) collective-permute-start(f32[2048,128]{1,0:T(8,128)S(1)} %convolution_add_fusion.1.refs_0_), channel_id=1, source_target_pairs={{0,2},{1,3},{2,0},{3,1},{4,6},{5,7},{6,4},{7,5},{8,10},{9,11},{10,... | collective-permute-start | bytes 3145736 | tf_op jit(solution)/shard_map/ppermute | solution.py:380
  35.6 0.6 dynamic-slice_bitcast_fusion.mix_ref
  36.3 0.0 copy-done
  36.3 13.4 %gram_sum_1.1 = f32[16,8,128]{2,1,0:T(8,128)} custom-call(f32[2048,128]{1,0:T(8,128)} %copy-done), custom_call_target="tpu_custom_call" | custom-call | tf_op jit(solution)/shard_map/gram_sum_1/pallas_call | solution.py:116
  49.7 6.1 %mixing_map.3 = f32[128,128]{1,0:T(8,128)} custom-call(f32[128,128]{1,0:T(8,128)} %bitcast.26, f32[128,128]{1,0:T(8,128)} %dynamic-slice_bitcast_fusion.mix_ref), custom_call_target="tpu_custom_call" | custom-call | tf_op jit(solution)/shard_map/mixing_map/pallas_call | solution.py:300
  55.8 0.5 collective-permute-start.3
  56.3 2.2 %fusion.2 = f32[2048,128]{1,0:T(8,128)S(1)} fusion(f32[2048,128]{1,0:T(8,128)} %copy-done, f32[128,128]{1,0:T(8,128)} %mixing_map.3), kind=kOutput, calls=%fused_computation.6 | convolution fusion | flops 402653184 | bytes 2162688 | tf_op jit(solution)/shard_map/dot_general | solution.py:373
  58.5 2.6 %collective-permute-done.3 = f32[128,128]{1,0:T(8,128)S(1)} collective-permute-done((f32[128,128]{1,0:T(8,128)}, f32[128,128]{1,0:T(8,128)S(1)}, u32[]{:S(2)}, u32[]{:S(2)}) %collective-permute-start.3) | collective-permute-done | bytes 65568 | tf_op jit(solution)/shard_map/ppermute | solution.py:380
  61.1 0.0 collective-permute-done.2
  61.1 1.9 %convolution_add_fusion.refs_0_ = f32[2048,128]{1,0:T(8,128)} fusion(f32[2048,128]{1,0:T(8,128)S(1)} %fusion.2, f32[2048,128]{1,0:T(8,128)S(1)} %collective-permute-done.2, f32[128,128]{1,0:T(8,128)S(1)} %collective-permute-done.3), kind=kOutput, calls=%fused_computation | convolution fusion | flops 402915328 | bytes 3211264 | tf_op jit(solution)/shard_map/dot_general | solution.py:373
  63.1 13.4 %gram_sum_2.1 = f32[16,8,128]{2,1,0:T(8,128)} custom-call(f32[2048,128]{1,0:T(8,128)} %convolution_add_fusion.refs_0_), custom_call_target="tpu_custom_call" | custom-call | tf_op jit(solution)/shard_map/gram_sum_2/pallas_call | solution.py:116
  76.5 5.7 %lower_inverse.1 = f32[128,128]{1,0:T(8,128)} custom-call(f32[128,128]{1,0:T(8,128)} %bitcast.27), custom_call_target="tpu_custom_call" | custom-call | tf_op jit(solution)/shard_map/lower_inverse/pallas_call | solution.py:290
  82.2 3.2 %fusion.3.own_ref = f32[2048,128]{1,0:T(8,128)} fusion(f32[2048,128]{1,0:T(8,128)} %convolution_add_fusion.refs_0_, f32[128,128]{1,0:T(8,128)} %lower_inverse.1), kind=kOutput, calls=%fused_computation.7 | convolution fusion | flops 402653184 | bytes 2162688 | tf_op jit(solution)/shard_map/dot_general | solution.py:369
  85.4 22.6 %basis_and_scores.1 = (f32[2,2048,128]{2,1,0:T(8,128)}, f32[128,128]{1,0:T(8,128)}) custom-call(bf16[1024,4096]{1,0:T(8,128)(2,1)} %get-tuple-element.7.centered_ref, f32[2048,128]{1,0:T(8,128)} %fusion.3.own_ref), custom_call_target="tpu_custom_call" | custom-call | tf_op jit(solution)/shard_map/basis_and_scores/pallas_call | solution.py:204
  107.9 3.0 %copy.7 = f32[1,4096,128]{2,1,0:T(8,128)} copy(f32[1,4096,128]{2,1,0:T(8,128)} %bitcast.23) | data formatting | bytes 4194304
  111.0 1.5 %copy.8 = f32[1,128,128]{2,1,0:T(8,128)} copy(f32[1,128,128]{2,1,0:T(8,128)} %bitcast.28) | data formatting | bytes 131072
  (1 shorter events, 0.0 us)
Async XLA Ops:
  0.6 23.5 %copy-start.1 = (f32[2,2,128,128]{3,2,1,0:T(8,128)S(1)}, f32[2,2,128,128]{3,2,1,0:T(8,128)}, u32[]{:S(2)}) copy-start(f32[2,2,128,128]{3,2,1,0:T(8,128)} %param.5) | copy-start | bytes 786436
  10.3 22.8 %collective-permute-start = (f32[2048,128]{1,0:T(8,128)}, f32[2048,128]{1,0:T(8,128)S(1)}, u32[]{:S(2)}, u32[]{:S(2)}) collective-permute-start(f32[2048,128]{1,0:T(8,128)} %get-tuple-element.9.refs_1_), channel_id=1, source_target_pairs={{0,1},{1,0},{2,3},{3,2},{4,5},{5,4},{6,7},{7,6},{8,9},{9,8},{10,11... | collective-permute-start | bytes 3145736 | tf_op jit(solution)/shard_map/ppermute | solution.py:380
  30.9 2.2 %collective-permute-start.1 = (f32[128,128]{1,0:T(8,128)}, f32[128,128]{1,0:T(8,128)S(1)}, u32[]{:S(2)}, u32[]{:S(2)}) collective-permute-start(f32[128,128]{1,0:T(8,128)} %mixing_map.2), channel_id=1, source_target_pairs={{0,1},{1,0},{2,3},{3,2},{4,5},{5,4},{6,7},{7,6},{8,9},{9,8},{10,11... | collective-permute-start | bytes 196616 | tf_op jit(solution)/shard_map/ppermute | solution.py:380
  34.1 2.2 %copy-start = (f32[2048,128]{1,0:T(8,128)}, f32[2048,128]{1,0:T(8,128)S(1)}, u32[]{:S(2)}) copy-start(f32[2048,128]{1,0:T(8,128)S(1)} %convolution_add_fusion.1.refs_0_) | copy-start | bytes 3145732
  34.1 27.0 %collective-permute-start.2 = (f32[2048,128]{1,0:T(8,128)S(1)}, f32[2048,128]{1,0:T(8,128)S(1)}, u32[]{:S(2)}, u32[]{:S(2)}) collective-permute-start(f32[2048,128]{1,0:T(8,128)S(1)} %convolution_add_fusion.1.refs_0_), channel_id=1, source_target_pairs={{0,2},{1,3},{2,0},{3,1},{4,6},{5,7},{6,4},{7,5},{8,10},{9,11},{10,... | collective-permute-start | bytes 3145736 | tf_op jit(solution)/shard_map/ppermute | solution.py:380
  55.8 5.3 %collective-permute-start.3 = (f32[128,128]{1,0:T(8,128)}, f32[128,128]{1,0:T(8,128)S(1)}, u32[]{:S(2)}, u32[]{:S(2)}) collective-permute-start(f32[128,128]{1,0:T(8,128)} %mixing_map.3), channel_id=1, source_target_pairs={{0,2},{1,3},{2,0},{3,1},{4,6},{5,7},{6,4},{7,5},{8,10},{9,11},{10,... | collective-permute-start | bytes 196616 | tf_op jit(solution)/shard_map/ppermute | solution.py:380
